TPU v7x, 32 devices: a whole 2x2x4 slice. The times are simulated.
32 devices in a mesh: rows: 8 (over y, x, core), cols: 4 (over z).
Axes of the slice: x: 2, y: 2, z: 4, core: 2. Of those that a mesh axis runs over, the one named last changes fastest.
Arguments:
- field: bfloat16 [32, 512, 512], P(None, 'rows', 'cols'), may hold values from -6 to 6
- cotangent: bfloat16 [32, 512, 512], P(None, 'rows', 'cols'), may hold values from -6 to 6
- weight_real: bfloat16 [32, 32, 8192], P(None, None, ('rows', 'cols')), may hold values from -0.75 to 0.75
- weight_imag: bfloat16 [32, 32, 8192], P(None, None, ('rows', 'cols')), may hold values from -0.75 to 0.75
- kernel: bfloat16 [3, 3, 32, 32], replicated, may hold values from -0.375 to 0.375
Outputs:
- layer_out: bfloat16 [32, 512, 512], P(None, 'rows', 'cols')
- field_grad: bfloat16 [32, 512, 512], P(None, 'rows', 'cols')
- weight_grad_real: float32 [32, 32, 8192], P(None, None, ('rows', 'cols'))
- weight_grad_imag: float32 [32, 32, 8192], P(None, None, ('rows', 'cols'))
- kernel_grad: float32 [3, 3, 32, 32], replicated
All inputs are finite; a program needn't handle non-finite values.
Results may differ from a plain program's by a relative error of at most 0.0068.
Values may be sent and summed in bfloat16 or wider, within the bound.
No kernel may reach another device: no remote copies, remote signals or barrier semaphores. Data moves between devices by JAX's collectives and lax.ppermute only.
A program may use at most 128 MiB of HBM per device.

v0:
```python
import math
import jax
import jax.numpy as jnp
from jax import lax
from jax.sharding import PartitionSpec as P

M = 64
highest = lax.Precision.HIGHEST


def padded_2(x, sides, width):
    for axis, dim in sides:
        devices, length = (lax.axis_size(axis), x.shape[dim])
        up = [(i, (i + 1) % devices) for i in range(devices - 1)]
        down = [(j, i) for i, j in up]
        last = lax.slice_in_dim(x, length - width, length, axis=dim)
        initial = lax.slice_in_dim(x, 0, width, axis=dim)
        before = lax.ppermute(last, axis, up)
        after = lax.ppermute(initial, axis, down)
        x = jnp.concatenate([before, x, after], axis=dim)
    return x


def tables(count_modes, offset, local, total):
    modes = jnp.arange(count_modes, dtype=jnp.int32)
    cells = offset + jnp.arange(local, dtype=jnp.int32)
    phase = modes[:, None] * cells[None, :] % total
    angle = phase.astype(jnp.float32) * (2.0 * math.pi / total)
    return (jnp.cos(angle), jnp.sin(angle))


def row_tables(count_modes, offset, local, total):
    base = jnp.arange(count_modes, dtype=jnp.int32)
    modes = jnp.concatenate([base, total - count_modes + base])
    cells = offset + jnp.arange(local, dtype=jnp.int32)
    phase = modes[:, None] * cells[None, :] % total
    angle = phase.astype(jnp.float32) * (2.0 * math.pi / total)
    return (jnp.cos(angle), jnp.sin(angle))


def exact(form, left, right):
    return jnp.einsum(form, left, right, precision=highest, preferred_element_type=jnp.float32)


def quick(form, left, right):
    return jnp.einsum(form, left, right, preferred_element_type=jnp.float32)


def smooth(values):
    return jax.nn.gelu(values, approximate=True)


def stencil(padded, weights):
    return lax.conv_general_dilated(
        padded[None], weights, (1, 1), ((0, 0), (0, 0)), preferred_element_type=jnp.float32
    )[0]


def owner_sums(partials):
    return lax.psum_scatter(partials, ("rows", "cols"), scatter_dimension=2, tiled=True)


def spread(owned):
    return lax.all_gather(owned, ("rows", "cols"), axis=2, tiled=True)


def rims(cells):
    return padded_2(cells, (("rows", 1), ("cols", 2)), 1)


def body(field, cotangent, weight_real, weight_imag, kernel):
    channels, rows_here, cols_here = field.shape
    total_rows = rows_here * lax.axis_size("rows")
    total_cols = cols_here * lax.axis_size("cols")
    cos_rows, sin_rows = row_tables(M, lax.axis_index("rows") * rows_here, rows_here, total_rows)
    cos_cols, sin_cols = tables(M, lax.axis_index("cols") * cols_here, cols_here, total_cols)
    scale_rows = 1.0 / math.sqrt(total_rows)
    scale_cols = 1.0 / math.sqrt(total_cols)
    scale_cells = 1.0 / math.sqrt(total_rows * total_cols)
    cos_cols_half = (cos_cols * scale_cols).astype(jnp.bfloat16)
    sin_cols_half = (-(sin_cols * scale_cols)).astype(jnp.bfloat16)
    half_real = quick("cij,bj->cib", field, cos_cols_half)
    half_imag = quick("cij,bj->cib", field, sin_cols_half)
    cos_rows_scaled = cos_rows * scale_rows
    sin_rows_scaled = sin_rows * scale_rows
    part_real = exact("ai,cib->cab", cos_rows_scaled, half_real) + exact(
        "ai,cib->cab", sin_rows_scaled, half_imag
    )
    part_imag = exact("ai,cib->cab", cos_rows_scaled, half_imag) - exact(
        "ai,cib->cab", sin_rows_scaled, half_real
    )
    owned = owner_sums(jnp.stack([part_real, part_imag]).reshape(2, channels, 2 * M * M))
    coef_real = owned[0]
    coef_imag = owned[1]
    wide_real = weight_real.astype(jnp.float32)
    wide_imag = weight_imag.astype(jnp.float32)
    mixed_real = exact("cm,com->om", coef_real, wide_real) - exact(
        "cm,com->om", coef_imag, wide_imag
    )
    mixed_imag = exact("cm,com->om", coef_real, wide_imag) + exact(
        "cm,com->om", coef_imag, wide_real
    )
    mixed = jnp.stack([mixed_real, mixed_imag]).astype(jnp.bfloat16)
    spectrum = spread(mixed).reshape(2, channels, 2 * M, M)
    cos_rows_half = cos_rows.astype(jnp.bfloat16)
    sin_rows_half = sin_rows.astype(jnp.bfloat16)
    back_real = quick("ai,oab->oib", cos_rows_half, spectrum[0]) - quick(
        "ai,oab->oib", sin_rows_half, spectrum[1]
    )
    back_imag = quick("ai,oab->oib", cos_rows_half, spectrum[1]) + quick(
        "ai,oab->oib", sin_rows_half, spectrum[0]
    )
    spectral = (
        exact("oib,bj->oij", back_real, cos_cols) - exact("oib,bj->oij", back_imag, sin_cols)
    ) / M
    padded = rims(field)
    forward_weights = jnp.transpose(kernel, (3, 2, 0, 1))
    preact = spectral + stencil(padded, forward_weights)
    activated, pullback = jax.vjp(smooth, preact)
    grad_pre = pullback(cotangent.astype(jnp.float32))[0].astype(jnp.bfloat16)
    cos_cols_plain = cos_cols.astype(jnp.bfloat16)
    sin_cols_plain = sin_cols.astype(jnp.bfloat16)
    grad_back_real = quick("oij,bj->oib", grad_pre, cos_cols_plain) / M
    grad_back_imag = -quick("oij,bj->oib", grad_pre, sin_cols_plain) / M
    grad_real = exact("ai,oib->oab", cos_rows, grad_back_real) + exact(
        "ai,oib->oab", sin_rows, grad_back_imag
    )
    grad_imag = exact("ai,oib->oab", cos_rows, grad_back_imag) - exact(
        "ai,oib->oab", sin_rows, grad_back_real
    )
    owned_grad = owner_sums(jnp.stack([grad_real, grad_imag]).reshape(2, channels, 2 * M * M))
    mode_real = owned_grad[0]
    mode_imag = owned_grad[1]
    weight_scale = M * scale_cells
    out_real = (
        coef_real[:, None, :] * mode_real[None] + coef_imag[:, None, :] * mode_imag[None]
    ) * weight_scale
    out_imag = (
        coef_real[:, None, :] * mode_imag[None] - coef_imag[:, None, :] * mode_real[None]
    ) * weight_scale
    input_real = exact("com,om->cm", wide_real, mode_real) + exact(
        "com,om->cm", wide_imag, mode_imag
    )
    input_imag = exact("com,om->cm", wide_real, mode_imag) - exact(
        "com,om->cm", wide_imag, mode_real
    )
    spectrum_grad = spread(jnp.stack([input_real, input_imag]).astype(jnp.bfloat16)).reshape(
        2, channels, 2 * M, M
    )
    cos_scaled_half = cos_rows_scaled.astype(jnp.bfloat16)
    sin_scaled_half = sin_rows_scaled.astype(jnp.bfloat16)
    line_real = quick("ai,cab->cib", cos_scaled_half, spectrum_grad[0]) - quick(
        "ai,cab->cib", sin_scaled_half, spectrum_grad[1]
    )
    line_imag = quick("ai,cab->cib", sin_scaled_half, spectrum_grad[0]) + quick(
        "ai,cab->cib", cos_scaled_half, spectrum_grad[1]
    )
    field_grad = exact("cib,bj->cij", line_real, cos_cols * scale_cols) - exact(
        "cib,bj->cij", line_imag, sin_cols * scale_cols
    )
    grad_padded = rims(grad_pre)
    backward_weights = jnp.transpose(kernel[::-1, ::-1], (2, 3, 0, 1))
    field_grad = field_grad + stencil(grad_padded, backward_weights)
    kernel_terms = []
    for row_step in range(3):
        for col_step in range(3):
            window = padded[:, row_step : row_step + rows_here, col_step : col_step + cols_here]
            kernel_terms.append(quick("cij,oij->co", window, grad_pre))
    kernel_local = jnp.stack(kernel_terms).reshape(3, 3, channels, channels)
    kernel_grad = lax.psum(kernel_local, ("rows", "cols")) * scale_cells
    return (
        activated.astype(jnp.bfloat16),
        field_grad.astype(jnp.bfloat16),
        out_real,
        out_imag,
        kernel_grad,
    )


def solution(mesh):
    placed = (
        P(None, "rows", "cols"),
        P(None, "rows", "cols"),
        P(None, None, ("rows", "cols")),
        P(None, None, ("rows", "cols")),
        P(),
    )
    return jax.shard_map(
        body,
        mesh=mesh,
        in_specs=placed,
        out_specs=(
            P(None, "rows", "cols"),
            P(None, "rows", "cols"),
            P(None, None, ("rows", "cols")),
            P(None, None, ("rows", "cols")),
            P(),
        ),
        check_vma=False,
    )
```

profile of v0, /device:TPU:0, one launch (start us, length us, event | category | flops | bytes accessed | tf_op | source)
XLA Modules:
  0.0 489.5 jit_solution(7288767995015641725)
XLA Ops:
  7.3 1.7 convolution_bitcast_fusion.1
  9.0 1.7 convolution_bitcast_fusion
  10.8 1.2 fusion.98
  11.9 1.2 fusion.100
  13.1 1.2 fusion.28
  14.3 2.1 fusion.29
  16.5 1.8 copy.175
  18.3 1.6 stack.72
  20.5 1.6 stack.73
  22.2 2.8 pad_maximum_fusion
  25.1 142.7 %reduce-scatter.3.cloned.1.call-done = f32[2,32,256]{2,1,0:T(8,128)} async-done(((f32[2,32,8192]{2,1,0:T(8,128)}), f32[2,32,256]{2,1,0:T(8,128)}) %reduce-scatter.3.cloned.1.call-update) | async-done | bytes 65552 | tf_op jit(solution)/shard_map/reduce_scatter | solution.py:60
  167.8 1.4 slice_bitcast_fusion.7
  170.7 1.3 collective-permute-start
  172.0 1.3 collective-permute-start.1
  173.7 1.4 collective-permute-done.1
  176.3 1.3 collective-permute-start.2
  178.3 1.5 collective-permute-start.3
  180.8 3.1 collective-permute-done.3
  185.5 2.7 copy.303
  188.3 1.4 pad.clone
  189.7 3.3 copy.192
  193.0 1.0 slice.124
  194.1 6.9 %broadcast_select_fusion.1 = f32[64,8,17,32]{3,1,2,0:T(8,128)} fusion(pred[8,17]{0,1:T(8,128)(4,1)S(1)} %copy-done.23, bf16[3,3,32,32]{3,2,1,0:T(8,128)(2,1)S(1)} %copy-done, bf16[32,66,1,7,2]{0,3,4,1,2:T(8,128)(2,1)S(1)} %slice.124, bf16[32,66,1,8,17]{0,3,4,1,2:T(8,128)(2,1)} %copy.192), kind=kOutput, calls=%fused_computation.16 | convolution fusion | flops 162636800 | bytes 1766280 | tf_op jit(solution)/shard_map/conv_general_dilated | solution.py:54
  201.0 4.4 copy.193
  205.4 1.5 slice.125
  206.9 3.7 copy.297
  210.7 10.7 %all-gather.3.cloned.1.call-done = bf16[2,32,8192]{2,1,0:T(8,128)(2,1)} async-done(((bf16[2,32,256]{2,1,0:T(8,128)(2,1)}), bf16[2,32,8192]{2,1,0:T(8,128)(2,1)}) %all-gather.3.cloned.1.call-update) | async-done | bytes 1048592 | tf_op jit(solution)/shard_map/all_gather | solution.py:64
  221.4 1.3 fusion.304
  222.7 1.1 squeeze.37
  223.8 1.1 squeeze.36
  226.9 1.8 fusion.94
  228.8 3.3 fusion.46
  233.0 1.8 fusion.91
  234.8 2.0 fusion.89
  236.8 2.8 fusion.24
  239.7 2.8 fusion.23
  242.5 1.8 copy.200
  244.3 1.6 stack.79
  246.0 1.8 copy.197
  247.8 1.6 stack.78
  249.4 3.0 pad_maximum_fusion.1
  253.2 2.1 collective-permute-start.4
  255.3 1.3 collective-permute-start.5
  260.7 132.0 %reduce-scatter.5.cloned.1.call-done = f32[2,32,256]{2,1,0:T(8,128)} async-done(((f32[2,32,8192]{2,1,0:T(8,128)}), f32[2,32,256]{2,1,0:T(8,128)}) %reduce-scatter.5.cloned.1.call-update) | async-done | bytes 65552 | tf_op jit(solution)/shard_map/reduce_scatter | solution.py:60
  392.7 1.4 slice_bitcast_fusion.3
  395.5 1.5 fusion.35
  397.7 39.6 %psum.7 = f32[3,3,32,32]{3,2,1,0:T(8,128)S(1)} all-reduce(f32[3,3,32,32]{3,2,1,0:T(8,128)S(1)} %bitcast.249), channel_id=1, replica_groups=mesh['rows'=8,'cols'=4] {'rows','cols'}, use_global_device_ids=true, to_apply=%region_2.3 | all-reduce | flops 9216 | bytes 73728 | tf_op jit(solution)/shard_map/psum | solution.py:170
  438.5 1.3 collective-permute-start.7
  439.8 5.4 %collective-permute-start.6 = (bf16[32,66,1]{1,0,2:T(8,128)(2,1)S(1)}, bf16[32,66,1]{1,0,2:T(8,128)(2,1)S(1)}, u32[]{:S(2)}, u32[]{:S(2)}) collective-permute-start(bf16[32,66,1]{1,0,2:T(8,128)(2,1)S(1)} %copy.207), channel_id=1, source_target_pairs={{0,1},{1,2},{2,3},{4,5},{5,6},{6,7},{8,9},{9,10},{10,11},{12,13},{... | collective-permute-start | bytes 12680 | tf_op jit(solution)/shard_map/ppermute | solution.py:18
  447.0 1.7 maximum_bitcast_fusion
  448.7 1.3 copy.304
  450.3 2.7 copy.213
  453.0 5.3 %broadcast_select_fusion = f32[64,8,17,32]{3,1,2,0:T(8,128)} fusion(pred[8,17]{0,1:T(8,128)(4,1)S(1)} %copy-done.24, bf16[3,3,32,32]{3,2,1,0:T(8,128)(2,1)S(1)} %copy-done, bf16[32,66,1,7,2]{0,3,4,1,2:T(8,128)(2,1)S(1)} %slice.134, bf16[32,66,1,8,17]{0,3,4,1,2:T(8,128)(2,1)S(1)} %copy.213), kind=kOutput, calls=%fused_computation.15 | convolution fusion | flops 162636800 | bytes 1766280 | tf_op jit(solution)/shard_map/conv_general_dilated | solution.py:54
  458.3 4.0 copy.214
  462.3 1.5 slice.135
  463.8 2.7 copy.298
  466.6 1.6 subtract_multiply_fusion
  468.2 2.1 fusion.303
  470.2 1.1 squeeze.41
  471.9 1.5 fusion.164
  473.4 2.3 squeeze.42
  475.7 1.7 fusion.22
  478.1 1.8 fusion.85
  479.9 2.7 fusion.32
  (115 shorter events, 21.2 us)
Async XLA Ops:
  7.2 186.9 %copy-start = (bf16[3,3,32,32]{3,2,1,0:T(8,128)(2,1)S(1)}, bf16[3,3,32,32]{3,2,1,0:T(8,128)(2,1)}, u32[]{:S(2)}) copy-start(bf16[3,3,32,32]{3,2,1,0:T(8,128)(2,1)} %param.9) | copy-start | bytes 55300
  7.2 160.6 %reduce-scatter.3.cloned.1.call-start = ((), (), s32[]{:S(2)}) async-start(), calls=%async_computation.2 | async-start | bytes 2162688 | tf_op jit(solution)/shard_map/reduce_scatter | solution.py:60
  7.3 225.3 %copy-start.19 = (s32[128]{0:T(128)}, s32[128]{0:T(128)S(1)}, u32[]{:S(2)}) copy-start(s32[128]{0:T(128)S(1)} %iota_add_fusion.2) | copy-start | bytes 1540
  20.5 1.6 copy-start.7
  25.0 144.2 %copy-start.8 = (bf16[32,32,256]{2,1,0:T(8,128)(2,1)S(1)}, bf16[32,32,256]{2,1,0:T(8,128)(2,1)}, u32[]{:S(2)}) copy-start(bf16[32,32,256]{2,1,0:T(8,128)(2,1)} %param.7) | copy-start | bytes 1572868
  25.0 144.2 %copy-start.10 = (bf16[32,32,256]{2,1,0:T(8,128)(2,1)S(1)}, bf16[32,32,256]{2,1,0:T(8,128)(2,1)}, u32[]{:S(2)}) copy-start(bf16[32,32,256]{2,1,0:T(8,128)(2,1)} %param.8) | copy-start | bytes 1572868
  25.0 145.3 %copy-start.1 = (bf16[32,64,128]{2,1,0:T(8,128)(2,1)S(1)}, bf16[32,64,128]{2,1,0:T(8,128)(2,1)}, u32[]{:S(2)}) copy-start(bf16[32,64,128]{2,1,0:T(8,128)(2,1)} %param.5) | copy-start | bytes 1572868
  25.0 196.4 %all-gather.3.cloned.1.call-start = ((), (), s32[]{:S(2)}) async-start(), calls=%async_computation.3 | async-start | bytes 1081344 | tf_op jit(solution)/shard_map/all_gather | solution.py:64
  170.2 222.4 %reduce-scatter.5.cloned.1.call-start = ((), (), s32[]{:S(2)}) async-start(), calls=%async_computation.4 | async-start | bytes 2162688 | tf_op jit(solution)/shard_map/reduce_scatter | solution.py:60
  170.6 4.4 copy-start.13
  170.7 2.6 collective-permute-start
  172.0 3.1 collective-permute-start.1
  175.0 0.6 copy-start.21
  176.3 3.5 collective-permute-start.2
  178.3 5.6 %collective-permute-start.3 = (bf16[32,66,1]{1,0,2:T(8,128)(2,1)S(1)}, bf16[32,66,1]{1,0,2:T(8,128)(2,1)S(1)}, u32[]{:S(2)}, u32[]{:S(2)}) collective-permute-start(bf16[32,66,1]{1,0,2:T(8,128)(2,1)S(1)} %copy.187), channel_id=1, source_target_pairs={{1,0},{2,1},{3,2},{5,4},{6,5},{7,6},{9,8},{10,9},{11,10},{13,12},{... | collective-permute-start | bytes 12680 | tf_op jit(solution)/shard_map/ppermute | solution.py:19
  180.8 7.5 %copy-start.5 = (bf16[32,66,1]{2,0,1:T(8,128)(2,1)}, bf16[32,66,1]{2,0,1:T(8,128)(2,1)S(1)}, u32[]{:S(2)}) copy-start(bf16[32,66,1]{2,0,1:T(8,128)(2,1)S(1)} %copy.188) | copy-start | bytes 12676
  184.8 3.4 copy-start.3
  189.7 4.4 copy-start.23
  226.4 2.4 copy-start.12
  226.4 2.4 copy-start.22
  252.5 4.2 copy-start.6
  252.5 4.7 copy-start.14
  252.5 5.1 %copy-start.4 = (bf16[32,66,1]{2,0,1:T(8,128)(2,1)S(1)}, bf16[32,66,1]{2,0,1:T(8,128)(2,1)}, u32[]{:S(2)}) copy-start(bf16[32,66,1]{2,0,1:T(8,128)(2,1)} %copy-done.3) | copy-start | bytes 12676
  252.5 215.7 %all-gather.5.cloned.1.call-start = ((), (), s32[]{:S(2)}) async-start(), calls=%async_computation.5 | async-start | bytes 1081344 | tf_op jit(solution)/shard_map/all_gather | solution.py:64
  253.2 184.1 %collective-permute-start.4 = (bf16[32,1,128]{2,1,0:T(2,128)(2,1)}, bf16[32,1,128]{2,1,0:T(2,128)(2,1)S(1)}, u32[]{:S(2)}, u32[]{:S(2)}) collective-permute-start(bf16[32,1,128]{2,1,0:T(2,128)(2,1)} %get-tuple-element.27), channel_id=1, source_target_pairs={{0,4},{4,8},{8,12},{12,16},{16,20},{20,24},{24,28},{1,5},{5,9},{9,... | collective-permute-start | bytes 24584 | tf_op jit(solution)/shard_map/ppermute | solution.py:18
  255.3 182.0 %collective-permute-start.5 = (bf16[32,1,128]{2,1,0:T(2,128)(2,1)}, bf16[32,1,128]{2,1,0:T(2,128)(2,1)S(1)}, u32[]{:S(2)}, u32[]{:S(2)}) collective-permute-start(bf16[32,1,128]{2,1,0:T(2,128)(2,1)} %get-tuple-element.28), channel_id=1, source_target_pairs={{4,0},{8,4},{12,8},{16,12},{20,16},{24,20},{28,24},{5,1},{9,5},{13... | collective-permute-start | bytes 24584 | tf_op jit(solution)/shard_map/ppermute | solution.py:19
  257.6 1.2 copy-start.2
  259.5 134.6 %copy-start.9 = (bf16[32,32,256]{2,1,0:T(8,128)(2,1)S(1)}, bf16[32,32,256]{2,1,0:T(8,128)(2,1)}, u32[]{:S(2)}) copy-start(bf16[32,32,256]{2,1,0:T(8,128)(2,1)} %param.7) | copy-start | bytes 1572868
  259.5 134.6 %copy-start.11 = (bf16[32,32,256]{2,1,0:T(8,128)(2,1)S(1)}, bf16[32,32,256]{2,1,0:T(8,128)(2,1)}, u32[]{:S(2)}) copy-start(bf16[32,32,256]{2,1,0:T(8,128)(2,1)} %param.8) | copy-start | bytes 1572868
  437.3 1.2 copy-start.18
  438.5 8.2 %collective-permute-start.7 = (bf16[32,66,1]{1,0,2:T(8,128)(2,1)S(1)}, bf16[32,66,1]{1,0,2:T(8,128)(2,1)S(1)}, u32[]{:S(2)}, u32[]{:S(2)}) collective-permute-start(bf16[32,66,1]{1,0,2:T(8,128)(2,1)S(1)} %copy.208), channel_id=1, source_target_pairs={{1,0},{2,1},{3,2},{5,4},{6,5},{7,6},{9,8},{10,9},{11,10},{13,12},{... | collective-permute-start | bytes 12680 | tf_op jit(solution)/shard_map/ppermute | solution.py:19
  439.8 6.5 %collective-permute-start.6 = (bf16[32,66,1]{1,0,2:T(8,128)(2,1)S(1)}, bf16[32,66,1]{1,0,2:T(8,128)(2,1)S(1)}, u32[]{:S(2)}, u32[]{:S(2)}) collective-permute-start(bf16[32,66,1]{1,0,2:T(8,128)(2,1)S(1)} %copy.207), channel_id=1, source_target_pairs={{0,1},{1,2},{2,3},{4,5},{5,6},{6,7},{8,9},{9,10},{10,11},{12,13},{... | collective-permute-start | bytes 12680 | tf_op jit(solution)/shard_map/ppermute | solution.py:18
  450.2 2.8 copy-start.24
  463.8 2.7 copy-start.15
  463.8 2.7 copy-start.16
  463.8 2.7 copy-start.17
  477.4 0.7 copy-start.20
Sparse Core Ops, SparseCore 0:
  25.1 142.6 reduce-scatter.2
  171.3 50.1 all-gather.2
  252.6 140.0 reduce-scatter.4
  395.7 50.0 all-gather.4
where the time goes:
time: 498 us; the launch traced here: 490 us
  waiting for transfers between devices  290 us (58%)
  local copies, waits for them, and re-layouts  62.2 us (12%)
  matrix products  53.5 us (11%)
  blocking collectives  39.6 us (8%)
  starting transfers between devices  15.6 us (3%)
  between operations  14.9 us (3%)
  other arithmetic  13.3 us (3%)
    reduce_scatter x2, waiting for transfers between devices, owner_sums(): lax.psum_scatter(partials, ('rows', 'cols'), scatter_dimension=2, tiled=T...  275 us
    psum x1, blocking collectives, body(): kernel_grad = lax.psum(kernel_local, ('rows', 'cols')) * scale_cells  39.6 us
    dot_general x12, matrix products, exact(): jnp.einsum(form, left, right, precision=highest, preferred_element_type=j...  24.8 us
    conv_general_dilated x8, local copies, waits for them, and re-layouts, stencil(): lax.conv_general_dilated(padded[None], weights, (1, 1), ((0, 0), (0, 0)),...  18.6 us
    dot_general x21, matrix products, quick(): return jnp.einsum(form, left, right, preferred_element_type=jnp.float32)  16.5 us
    conv_general_dilated x2, matrix products, stencil(): lax.conv_general_dilated(padded[None], weights, (1, 1), ((0, 0), (0, 0)),...  12.2 us
    unnamed x57, local copies, waits for them, and re-layouts  11.8 us
    all_gather x2, waiting for transfers between devices, spread(): return lax.all_gather(owned, ('rows', 'cols'), axis=2, tiled=True)  10.7 us
  transfers between devices with their start and end apart: 12, of which 6 were waited for; matrix products, arithmetic and copies ran while one was open for 13% of the time, Pallas kernels for 0%

commit v1 on v0

--- a/solution.py
+++ b/solution.py
@@ -167,7 +167,7 @@
             window = padded[:, row_step : row_step + rows_here, col_step : col_step + cols_here]
             kernel_terms.append(quick("cij,oij->co", window, grad_pre))
     kernel_local = jnp.stack(kernel_terms).reshape(3, 3, channels, channels)
-    kernel_grad = lax.psum(kernel_local, ("rows", "cols")) * scale_cells
+    kernel_grad = jnp.sum(lax.all_gather(kernel_local, ("rows", "cols")), axis=0) * scale_cells
     return (
         activated.astype(jnp.bfloat16),
         field_grad.astype(jnp.bfloat16),

time: 498 us -> 542 us (1.088)
  waiting for transfers between devices: 290 us -> 374 us
  blocking collectives: 39.6 us -> 0 us
    all_gather x2, waiting for transfers between devices: 10.7 us -> 59.2 us  [spread(): return lax.all_gather(owned, ('rows', 'cols'), axis=2, tiled=True)]
    psum x1 -> x0, blocking collectives: 39.6 us -> none  [body(): kernel_grad = lax.psum(kernel_local, ('rows', 'cols')) * scale_cells]
    all_gather x0 -> x1, waiting for transfers between devices: none -> 27.7 us  [body(): lax.all_gather(kernel_local, ('rows', 'cols'))]
    ppermute x4, waiting for transfers between devices: 4.48 us -> 10 us  [padded_2(): after = lax.ppermute(initial, axis, down)]
    unnamed x57 -> x51, local copies, waits for them, and re-layouts: 11.8 us -> 12.2 us
  transfers between devices with their start and end apart: 12 -> 13, of which waited for: 6 -> 9; matrix products, arithmetic and copies ran while one was open for 13% -> 12% of each run, Pallas kernels for 0% -> 0%
where the time goes in v1:
time: 542 us; the launch traced here: 533 us
  waiting for transfers between devices  374 us (69%)
  local copies, waits for them, and re-layouts  63.5 us (12%)
  matrix products  54.3 us (10%)
  other arithmetic  15.6 us (3%)
  between operations  14.9 us (3%)
  starting transfers between devices  10.9 us (2%)
    reduce_scatter x2, waiting for transfers between devices, owner_sums(): lax.psum_scatter(partials, ('rows', 'cols'), scatter_dimension=2, tiled=T...  277 us
    all_gather x2, waiting for transfers between devices, spread(): return lax.all_gather(owned, ('rows', 'cols'), axis=2, tiled=True)  59.2 us
    all_gather x1, waiting for transfers between devices, body(): lax.all_gather(kernel_local, ('rows', 'cols'))  27.7 us
    dot_general x12, matrix products, exact(): jnp.einsum(form, left, right, precision=highest, preferred_element_type=j...  25.8 us
    conv_general_dilated x8, local copies, waits for them, and re-layouts, stencil(): lax.conv_general_dilated(padded[None], weights, (1, 1), ((0, 0), (0, 0)),...  20.1 us
    dot_general x21, matrix products, quick(): return jnp.einsum(form, left, right, preferred_element_type=jnp.float32)  15.4 us
    conv_general_dilated x2, matrix products, stencil(): lax.conv_general_dilated(padded[None], weights, (1, 1), ((0, 0), (0, 0)),...  13.1 us
    unnamed x51, local copies, waits for them, and re-layouts  12.2 us
  transfers between devices with their start and end apart: 13, of which 9 were waited for; matrix products, arithmetic and copies ran while one was open for 12% of the time, Pallas kernels for 0%

profile of v1, /device:TPU:0, one launch (start us, length us, event | category | flops | bytes accessed | tf_op | source)
XLA Modules:
  0.0 532.9 jit_solution(5552376700054556673)
XLA Ops:
  7.3 1.7 convolution_bitcast_fusion.1
  9.0 1.7 convolution_bitcast_fusion
  10.8 1.2 fusion.98
  11.9 1.2 fusion.100
  13.1 2.1 fusion.28
  15.2 2.1 fusion.29
  17.4 1.8 copy.175
  19.2 1.6 stack.72
  21.5 1.6 stack.73
  23.1 2.8 pad_maximum_fusion
  26.0 143.1 %reduce-scatter.3.cloned.1.call-done = f32[2,32,256]{2,1,0:T(8,128)} async-done(((f32[2,32,8192]{2,1,0:T(8,128)}), f32[2,32,256]{2,1,0:T(8,128)}) %reduce-scatter.3.cloned.1.call-update) | async-done | bytes 65552 | tf_op jit(solution)/shard_map/reduce_scatter | solution.py:60
  169.1 1.4 slice_bitcast_fusion.7
  172.0 1.3 collective-permute-start
  173.3 1.3 collective-permute-start.1
  175.0 1.4 collective-permute-done.1
  177.2 1.3 collective-permute-start.2
  179.2 1.5 collective-permute-start.3
  181.7 3.1 collective-permute-done.3
  186.4 2.7 copy.303
  189.1 1.4 pad.clone
  190.6 3.3 copy.192
  194.9 7.0 %broadcast_select_fusion.1 = f32[64,8,17,32]{3,1,2,0:T(8,128)} fusion(pred[8,17]{0,1:T(8,128)(4,1)S(1)} %copy-done.21, bf16[3,3,32,32]{3,2,1,0:T(8,128)(2,1)S(1)} %copy-done, bf16[32,66,1,7,2]{0,3,4,1,2:T(8,128)(2,1)S(1)} %slice.124, bf16[32,66,1,8,17]{0,3,4,1,2:T(8,128)(2,1)} %copy.192), kind=kOutput, calls=%fused_computation.16 | convolution fusion | flops 162636800 | bytes 1766280 | tf_op jit(solution)/shard_map/conv_general_dilated | solution.py:54
  201.9 4.4 copy.193
  206.4 1.5 slice.125
  207.8 3.6 copy.297
  211.5 11.0 %all-gather.4.cloned.1.call-done = bf16[2,32,8192]{2,1,0:T(8,128)(2,1)} async-done(((bf16[2,32,256]{2,1,0:T(8,128)(2,1)}), bf16[2,32,8192]{2,1,0:T(8,128)(2,1)}) %all-gather.4.cloned.1.call-update) | async-done | bytes 1048592 | tf_op jit(solution)/shard_map/all_gather | solution.py:64
  222.5 1.3 fusion.304
  223.8 1.1 squeeze.37
  224.9 1.1 squeeze.36
  228.0 1.8 fusion.94
  229.9 3.3 fusion.46
  234.0 1.8 fusion.91
  235.9 2.0 fusion.89
  237.9 2.8 fusion.24
  240.7 2.8 fusion.23
  243.6 1.8 copy.200
  245.4 1.6 stack.79
  247.0 1.8 copy.197
  248.9 1.6 stack.78
  250.5 3.1 pad_maximum_fusion.1
  260.1 133.6 %reduce-scatter.5.cloned.1.call-done = f32[2,32,256]{2,1,0:T(8,128)} async-done(((f32[2,32,8192]{2,1,0:T(8,128)}), f32[2,32,256]{2,1,0:T(8,128)}) %reduce-scatter.5.cloned.1.call-update) | async-done | bytes 65552 | tf_op jit(solution)/shard_map/reduce_scatter | solution.py:60
  393.7 1.4 slice_bitcast_fusion.3
  396.6 1.3 collective-permute-start.4
  397.9 1.3 collective-permute-start.5
  399.2 1.8 collective-permute-done.5
  401.8 1.3 collective-permute-start.6
  403.4 1.3 collective-permute-start.7
  405.1 3.9 collective-permute-done.7
  410.4 1.3 copy.304
  411.9 3.3 copy.213
  416.2 6.1 %broadcast_select_fusion = f32[64,8,17,32]{3,1,2,0:T(8,128)} fusion(pred[8,17]{0,1:T(8,128)(4,1)S(1)} %copy-done.21, bf16[3,3,32,32]{3,2,1,0:T(8,128)(2,1)S(1)} %copy-done, bf16[32,66,1,7,2]{0,3,4,1,2:T(8,128)(2,1)S(1)} %slice.134, bf16[32,66,1,8,17]{0,3,4,1,2:T(8,128)(2,1)} %copy.213), kind=kOutput, calls=%fused_computation.15 | convolution fusion | flops 162636800 | bytes 1766280 | tf_op jit(solution)/shard_map/conv_general_dilated | solution.py:54
  422.4 4.0 copy.214
  426.4 1.5 slice.135
  427.9 2.7 copy.298
  430.6 27.7 %all-gather.8.cloned.1.call-done = f32[32,3,3,32,32]{4,3,2,1,0:T(8,128)} async-done(((f32[1,3,3,32,32]{4,3,2,1,0:T(8,128)}), f32[32,3,3,32,32]{4,3,2,1,0:T(8,128)}) %all-gather.8.cloned.1.call-update) | async-done | bytes 1179664 | tf_op jit(solution)/shard_map/all_gather | solution.py:170
  458.3 2.9 reduce_sum.9
  462.0 1.6 subtract_multiply_fusion
  463.6 48.1 %all-gather.6.cloned.1.call-done = bf16[2,32,8192]{2,1,0:T(8,128)(2,1)} async-done(((bf16[2,32,256]{2,1,0:T(8,128)(2,1)}), bf16[2,32,8192]{2,1,0:T(8,128)(2,1)}) %all-gather.6.cloned.1.call-update) | async-done | bytes 1048592 | tf_op jit(solution)/shard_map/all_gather | solution.py:64
  511.7 2.1 fusion.303
  515.4 1.5 fusion.164
  516.9 2.3 squeeze.42
  519.2 1.7 fusion.22
  521.4 1.8 fusion.85
  523.3 2.7 fusion.32
  (112 shorter events, 25.5 us)
Async XLA Ops:
  7.2 187.8 %copy-start = (bf16[3,3,32,32]{3,2,1,0:T(8,128)(2,1)S(1)}, bf16[3,3,32,32]{3,2,1,0:T(8,128)(2,1)}, u32[]{:S(2)}) copy-start(bf16[3,3,32,32]{3,2,1,0:T(8,128)(2,1)} %param.9) | copy-start | bytes 55300
  7.2 161.9 %reduce-scatter.3.cloned.1.call-start = ((), (), s32[]{:S(2)}) async-start(), calls=%async_computation.2 | async-start | bytes 2162688 | tf_op jit(solution)/shard_map/reduce_scatter | solution.py:60
  19.2 1.6 copy-start.7
  21.5 1.6 copy-start.8
  25.9 144.6 %copy-start.9 = (bf16[32,32,256]{2,1,0:T(8,128)(2,1)S(1)}, bf16[32,32,256]{2,1,0:T(8,128)(2,1)}, u32[]{:S(2)}) copy-start(bf16[32,32,256]{2,1,0:T(8,128)(2,1)} %param.7) | copy-start | bytes 1572868
  25.9 144.6 %copy-start.11 = (bf16[32,32,256]{2,1,0:T(8,128)(2,1)S(1)}, bf16[32,32,256]{2,1,0:T(8,128)(2,1)}, u32[]{:S(2)}) copy-start(bf16[32,32,256]{2,1,0:T(8,128)(2,1)} %param.8) | copy-start | bytes 1572868
  25.9 145.6 %copy-start.1 = (bf16[32,64,128]{2,1,0:T(8,128)(2,1)S(1)}, bf16[32,64,128]{2,1,0:T(8,128)(2,1)}, u32[]{:S(2)}) copy-start(bf16[32,64,128]{2,1,0:T(8,128)(2,1)} %param.5) | copy-start | bytes 1572868
  26.0 196.5 %all-gather.4.cloned.1.call-start = ((), (), s32[]{:S(2)}) async-start(), calls=%async_computation.3 | async-start | bytes 1081344 | tf_op jit(solution)/shard_map/all_gather | solution.py:64
  171.5 222.2 %reduce-scatter.5.cloned.1.call-start = ((), (), s32[]{:S(2)}) async-start(), calls=%async_computation.4 | async-start | bytes 2162688 | tf_op jit(solution)/shard_map/reduce_scatter | solution.py:60
  171.9 2.6 copy-start.14
  172.0 2.6 collective-permute-start
  173.3 3.1 collective-permute-start.1
  177.2 3.5 collective-permute-start.2
  179.2 5.5 %collective-permute-start.3 = (bf16[32,66,1]{1,0,2:T(8,128)(2,1)S(1)}, bf16[32,66,1]{1,0,2:T(8,128)(2,1)S(1)}, u32[]{:S(2)}, u32[]{:S(2)}) collective-permute-start(bf16[32,66,1]{1,0,2:T(8,128)(2,1)S(1)} %copy.187), channel_id=1, source_target_pairs={{1,0},{2,1},{3,2},{5,4},{6,5},{7,6},{9,8},{10,9},{11,10},{13,12},{... | collective-permute-start | bytes 12680 | tf_op jit(solution)/shard_map/ppermute | solution.py:19
  181.7 7.4 %copy-start.5 = (bf16[32,66,1]{2,0,1:T(8,128)(2,1)}, bf16[32,66,1]{2,0,1:T(8,128)(2,1)S(1)}, u32[]{:S(2)}) copy-start(bf16[32,66,1]{2,0,1:T(8,128)(2,1)S(1)} %copy.188) | copy-start | bytes 12676
  185.7 3.4 copy-start.3
  190.6 4.4 copy-start.21
  227.5 2.4 copy-start.13
  227.5 2.4 copy-start.20
  250.5 3.2 copy-start.6
  253.6 1.0 copy-start.15
  253.6 1.5 copy-start.4
  253.6 204.7 %all-gather.8.cloned.1.call-start = ((), (), s32[]{:S(2)}) async-start(), calls=%async_computation.6 | async-start | bytes 4866048 | tf_op jit(solution)/shard_map/all_gather | solution.py:170
  255.1 1.2 copy-start.2
  258.1 137.0 %copy-start.10 = (bf16[32,32,256]{2,1,0:T(8,128)(2,1)S(1)}, bf16[32,32,256]{2,1,0:T(8,128)(2,1)}, u32[]{:S(2)}) copy-start(bf16[32,32,256]{2,1,0:T(8,128)(2,1)} %param.7) | copy-start | bytes 1572868
  258.1 137.0 %copy-start.12 = (bf16[32,32,256]{2,1,0:T(8,128)(2,1)S(1)}, bf16[32,32,256]{2,1,0:T(8,128)(2,1)}, u32[]{:S(2)}) copy-start(bf16[32,32,256]{2,1,0:T(8,128)(2,1)} %param.8) | copy-start | bytes 1572868
  259.2 0.7 copy-start.16
  259.9 251.9 %all-gather.6.cloned.1.call-start = ((), (), s32[]{:S(2)}) async-start(), calls=%async_computation.5 | async-start | bytes 1081344 | tf_op jit(solution)/shard_map/all_gather | solution.py:64
  396.6 2.6 collective-permute-start.4
  397.9 3.1 collective-permute-start.5
  401.8 2.9 collective-permute-start.6
  403.4 5.5 %collective-permute-start.7 = (bf16[32,66,1]{1,0,2:T(8,128)(2,1)S(1)}, bf16[32,66,1]{1,0,2:T(8,128)(2,1)S(1)}, u32[]{:S(2)}, u32[]{:S(2)}) collective-permute-start(bf16[32,66,1]{1,0,2:T(8,128)(2,1)S(1)} %copy.208), channel_id=1, source_target_pairs={{1,0},{2,1},{3,2},{5,4},{6,5},{7,6},{9,8},{10,9},{11,10},{13,12},{... | collective-permute-start | bytes 12680 | tf_op jit(solution)/shard_map/ppermute | solution.py:19
  430.6 31.4 %copy-start.17 = (f32[32,256]{1,0:T(8,128)S(1)}, f32[32,256]{1,0:T(8,128)}, u32[]{:S(2)}) copy-start(f32[32,256]{1,0:T(8,128)} %get-tuple-element.36) | copy-start | bytes 98308
  430.6 31.3 %copy-start.18 = (f32[32,256]{1,0:T(8,128)S(1)}, f32[32,256]{1,0:T(8,128)}, u32[]{:S(2)}) copy-start(f32[32,256]{1,0:T(8,128)} %get-tuple-element.37) | copy-start | bytes 98308
  430.6 31.3 %copy-start.19 = (f32[32,256]{1,0:T(8,128)S(1)}, f32[32,256]{1,0:T(8,128)}, u32[]{:S(2)}) copy-start(f32[32,256]{1,0:T(8,128)} %get-tuple-element.40) | copy-start | bytes 98308
Sparse Core Ops, SparseCore 0:
  26.1 142.9 reduce-scatter.2
  172.6 49.8 all-gather.3
  253.7 139.9 reduce-scatter.4
  397.0 61.3 all-gather.7
  461.1 50.5 all-gather.5
